TPU v7x, 32 devices: a whole 2x2x4 slice. The times are simulated.
32 devices in a mesh: prow: 4 (over y, core), pcol: 8 (over z, x).
Axes of the slice: x: 2, y: 2, z: 4, core: 2. Of those that a mesh axis runs over, the one named last changes fastest.
Arguments:
- right_side: float32 [8, 256, 128], P(None, 'prow'), may hold values from -6 to 6
- lower_prev: float32 [8, 256, 129024], P(None, 'prow', 'pcol'), may hold values from -0.015625 to 0.015625
- solved_prev: float32 [129024, 128], P('pcol'), may hold values from -6 to 6
- lower_window: float32 [8, 256, 2048], P(None, 'prow', 'pcol'), may hold values from -0.1875 to 0.1875
- inverse_diag: float32 [8, 256, 256], P(None, 'prow'), may hold values from -0.25 to 1.4, as said below
Outputs:
- solution: float32 [8, 256, 128], P(None, 'prow')
Inputs may be any that keep to these rules, and one draw needn't show every extreme that they name: `inverse_diag`: each block is lower triangular: zero above its diagonal, with diagonal entries of 0.7 to 1.4.
All inputs are finite; a program needn't handle non-finite values.
Results may differ from a plain program's by a relative error of at most 0.00011.
Values sent between devices are 32-bit elements; how exact they have to be, the bound alone decides.
No kernel may reach another device: no remote copies, remote signals or barrier semaphores. Data moves between devices by JAX's collectives and lax.ppermute only.
A program may use at most 128 MiB of HBM per device.

v0:
```python
import jax
import jax.numpy as jnp
from jax import lax
from jax.sharding import PartitionSpec as P


def local(right_side, lower_prev, solved_prev, lower_window, inverse_diag):
    highest = lax.Precision.HIGHEST
    blocks = right_side.shape[0]
    local_rows = right_side.shape[1]
    columns = right_side.shape[2]
    block_rows = inverse_diag.shape[2]
    row_start = lax.axis_index("prow") * local_rows
    solved = jnp.zeros((blocks * block_rows, columns), jnp.float32)
    pieces = []
    full_inverse = lax.all_gather(inverse_diag, "prow", axis=1, tiled=True)
    full_window = lax.all_gather(lower_window, "pcol", axis=2, tiled=True)
    for row_block in range(blocks):
        window_term = jnp.dot(
            full_window[row_block], solved, precision=highest, preferred_element_type=jnp.float32
        )
        earlier_part = jnp.dot(
            lower_prev[row_block],
            solved_prev,
            precision=highest,
            preferred_element_type=jnp.float32,
        )
        earlier_here = lax.psum(earlier_part, "pcol")
        local_residual = right_side[row_block] - (earlier_here + window_term)
        residual = lax.all_gather(local_residual, "prow", axis=0, tiled=True)
        whole_rows = jnp.dot(
            full_inverse[row_block], residual, precision=highest, preferred_element_type=jnp.float32
        )
        pieces.append(lax.dynamic_slice_in_dim(whole_rows, row_start, local_rows, 0))
        solved = lax.dynamic_update_slice_in_dim(solved, whole_rows, row_block * block_rows, 0)
    return jnp.stack(pieces)


def solution(mesh):
    in_specs = (
        P(None, "prow", None),
        P(None, "prow", "pcol"),
        P("pcol", None),
        P(None, "prow", "pcol"),
        P(None, "prow", None),
    )
    out_specs = P(None, "prow", None)
    return jax.shard_map(local, mesh=mesh, in_specs=in_specs, out_specs=out_specs, check_vma=False)
```

profile of v0, /device:TPU:0, one launch (start us, length us, event | category | flops | bytes accessed | tf_op | source)
XLA Modules:
  0.0 249.5 jit_solution(15784132453054589347)
XLA Ops:
  6.5 0.7 all-gather.3.cloned.1.call-update
  7.3 10.3 %fusion.4 = f32[64,128]{1,0:T(8,128)} fusion(f32[16128,128]{1,0:T(8,128)} %param.7, f32[8,64,16128]{2,1,0:T(8,128)} %param.6), kind=kOutput, calls=%fused_computation.4 | convolution fusion | flops 1585446912 | bytes 12419072 | tf_op jit(solution)/shard_map/dot_general | solution.py:22
  17.7 8.1 %fusion.6 = f32[64,128]{1,0:T(8,128)} fusion(f32[16128,128]{1,0:T(8,128)S(1)} %copy-done, f32[8,64,16128]{2,1,0:T(8,128)} %param.6), kind=kOutput, calls=%fused_computation.6 | convolution fusion | flops 1585446912 | bytes 12419072 | tf_op jit(solution)/shard_map/dot_general | solution.py:22
  25.8 7.9 %fusion.8 = f32[64,128]{1,0:T(8,128)} fusion(f32[16128,128]{1,0:T(8,128)S(1)} %copy-done, f32[8,64,16128]{2,1,0:T(8,128)} %param.6), kind=kOutput, calls=%fused_computation.8 | convolution fusion | flops 1585446912 | bytes 12419072 | tf_op jit(solution)/shard_map/dot_general | solution.py:22
  33.7 8.1 %fusion.10 = f32[64,128]{1,0:T(8,128)} fusion(f32[16128,128]{1,0:T(8,128)S(1)} %copy-done, f32[8,64,16128]{2,1,0:T(8,128)} %param.6), kind=kOutput, calls=%fused_computation.10 | convolution fusion | flops 1585446912 | bytes 12419072 | tf_op jit(solution)/shard_map/dot_general | solution.py:22
  41.8 7.9 %fusion.12 = f32[64,128]{1,0:T(8,128)} fusion(f32[16128,128]{1,0:T(8,128)S(1)} %copy-done, f32[8,64,16128]{2,1,0:T(8,128)} %param.6), kind=kOutput, calls=%fused_computation.12 | convolution fusion | flops 1585446912 | bytes 12419072 | tf_op jit(solution)/shard_map/dot_general | solution.py:22
  49.7 8.4 %fusion.14 = f32[64,128]{1,0:T(8,128)} fusion(f32[16128,128]{1,0:T(8,128)S(1)} %copy-done, f32[8,64,16128]{2,1,0:T(8,128)} %param.6), kind=kOutput, calls=%fused_computation.14 | convolution fusion | flops 1585446912 | bytes 12419072 | tf_op jit(solution)/shard_map/dot_general | solution.py:22
  58.1 7.9 %fusion = f32[64,128]{1,0:T(8,128)} fusion(f32[16128,128]{1,0:T(8,128)S(1)} %copy-done, f32[8,64,16128]{2,1,0:T(8,128)} %param.6), kind=kOutput, calls=%fused_computation | convolution fusion | flops 1585446912 | bytes 12419072 | tf_op jit(solution)/shard_map/dot_general | solution.py:22
  66.1 8.2 %fusion.2 = f32[64,128]{1,0:T(8,128)} fusion(f32[16128,128]{1,0:T(8,128)S(1)} %copy-done, f32[8,64,16128]{2,1,0:T(8,128)} %param.6), kind=kOutput, calls=%fused_computation.2 | convolution fusion | flops 1585446912 | bytes 12419072 | tf_op jit(solution)/shard_map/dot_general | solution.py:22
  74.3 0.7 all-gather.5.cloned.1.call-update
  75.0 12.2 %all-gather.3.cloned.1.call-done = f32[8,64,2048]{2,1,0:T(8,128)} async-done(((f32[8,64,256]{2,1,0:T(8,128)}), f32[8,64,2048]{2,1,0:T(8,128)}) %all-gather.3.cloned.1.call-update) | async-done | bytes 4194320 | tf_op jit(solution)/shard_map/all_gather | solution.py:17
  87.1 1.2 fusion.38
  88.3 73.8 %all-reduce.4.cloned.1.call-done = (f32[64,128]{1,0:T(8,128)}, f32[64,128]{1,0:T(8,128)}, f32[64,128]{1,0:T(8,128)}, f32[64,128]{1,0:T(8,128)}, f32[64,128]{1,0:...) async-done(((f32[64,128]{1,0:T(8,128)}, f32[64,128]{1,0:T(8,128)}, f32[64,128]{1,0:T(8,128)}, f32[64,128]{1,0:T(8,128)}, f32[64,128]{1,0:T(8,128)}, ...) | async-done | bytes 262160 | tf_op jit(solution)/shard_map/psum | solution.py:28
  162.1 0.8 bitcast_subtract_fusion
  163.0 5.4 %all_gather.31 = f32[256,128]{1,0:T(8,128)S(1)} all-gather(f32[64,128]{1,0:T(8,128)S(1)} %bitcast_subtract_fusion), channel_id=1, replica_groups=mesh['prow'=4,'pcol'=8] {'prow'}, dimensions={0}, use_global_device_ids=true | all-gather | bytes 163840 | tf_op jit(solution)/shard_map/all_gather | solution.py:30
  168.4 17.4 %all-gather.5.cloned.1.call-done = f32[8,256,256]{2,1,0:T(8,128)} async-done(((f32[8,64,256]{2,1,0:T(8,128)}), f32[8,256,256]{2,1,0:T(8,128)}) %all-gather.5.cloned.1.call-update) | async-done | bytes 2097168 | tf_op jit(solution)/shard_map/all_gather | solution.py:16
  185.8 1.5 fusion.47
  187.3 2.1 fusion.25
  189.4 5.4 %all_gather.33 = f32[256,128]{1,0:T(8,128)S(1)} all-gather(f32[64,128]{1,0:T(8,128)S(1)} %fusion.25), channel_id=1, replica_groups=mesh['prow'=4,'pcol'=8] {'prow'}, dimensions={0}, use_global_device_ids=true | all-gather | bytes 163840 | tf_op jit(solution)/shard_map/all_gather | solution.py:30
  194.8 0.1 bitcast_dynamic-update-slice_fusion.13
  194.9 0.1 dynamic_update_slice.21
  195.0 1.4 bitcast_dynamic-update-slice_fusion.5
  196.4 2.3 fusion.27
  198.7 5.4 %all_gather.34 = f32[256,128]{1,0:T(8,128)S(1)} all-gather(f32[64,128]{1,0:T(8,128)S(1)} %fusion.27), channel_id=1, replica_groups=mesh['prow'=4,'pcol'=8] {'prow'}, dimensions={0}, use_global_device_ids=true | all-gather | bytes 163840 | tf_op jit(solution)/shard_map/all_gather | solution.py:30
  204.1 1.4 bitcast_dynamic-update-slice_fusion.4
  205.5 1.2 fusion.29
  206.7 5.6 %all_gather.35 = f32[256,128]{1,0:T(8,128)S(1)} all-gather(f32[64,128]{1,0:T(8,128)S(1)} %fusion.29), channel_id=1, replica_groups=mesh['prow'=4,'pcol'=8] {'prow'}, dimensions={0}, use_global_device_ids=true | all-gather | bytes 163840 | tf_op jit(solution)/shard_map/all_gather | solution.py:30
  212.3 0.4 bitcast_dynamic-update-slice_fusion.3
  212.7 1.2 fusion.31
  213.9 5.4 %all_gather.36 = f32[256,128]{1,0:T(8,128)S(1)} all-gather(f32[64,128]{1,0:T(8,128)S(1)} %fusion.31), channel_id=1, replica_groups=mesh['prow'=4,'pcol'=8] {'prow'}, dimensions={0}, use_global_device_ids=true | all-gather | bytes 163840 | tf_op jit(solution)/shard_map/all_gather | solution.py:30
  219.4 0.4 bitcast_dynamic-update-slice_fusion.2
  219.8 1.2 fusion.33
  221.0 5.4 %all_gather.37 = f32[256,128]{1,0:T(8,128)S(1)} all-gather(f32[64,128]{1,0:T(8,128)S(1)} %fusion.33), channel_id=1, replica_groups=mesh['prow'=4,'pcol'=8] {'prow'}, dimensions={0}, use_global_device_ids=true | all-gather | bytes 163840 | tf_op jit(solution)/shard_map/all_gather | solution.py:30
  226.4 0.4 bitcast_dynamic-update-slice_fusion.1
  226.9 1.2 fusion.35
  228.1 5.6 %all_gather.38 = f32[256,128]{1,0:T(8,128)S(1)} all-gather(f32[64,128]{1,0:T(8,128)S(1)} %fusion.35), channel_id=1, replica_groups=mesh['prow'=4,'pcol'=8] {'prow'}, dimensions={0}, use_global_device_ids=true | all-gather | bytes 163840 | tf_op jit(solution)/shard_map/all_gather | solution.py:30
  233.7 0.4 bitcast_dynamic-update-slice_fusion
  234.2 1.2 fusion.37
  235.4 5.4 %all_gather.39 = f32[256,128]{1,0:T(8,128)S(1)} all-gather(f32[64,128]{1,0:T(8,128)S(1)} %fusion.37), channel_id=1, replica_groups=mesh['prow'=4,'pcol'=8] {'prow'}, dimensions={0}, use_global_device_ids=true | all-gather | bytes 163840 | tf_op jit(solution)/shard_map/all_gather | solution.py:30
  240.8 0.1 bitcast_dynamic-update-slice_fusion.12
  240.9 0.1 bitcast_dynamic-update-slice_fusion.11
  241.0 0.1 bitcast_dynamic-update-slice_fusion.10
  241.1 0.1 bitcast_dynamic-update-slice_fusion.9
  241.2 0.1 bitcast_dynamic-update-slice_fusion.8
  241.2 0.1 bitcast_dynamic-update-slice_fusion.7
  241.3 0.4 fusion.40
  241.7 0.1 bitcast_dynamic-update-slice_fusion.6
  241.8 0.9 copy.7
  (22 shorter events, 0.1 us)
Async XLA Ops:
  6.5 80.6 %all-gather.3.cloned.1.call-start = ((), (), s32[]{:S(2)}) async-start(), calls=%async_computation | async-start | bytes 4718592 | tf_op jit(solution)/shard_map/all_gather | solution.py:17
  7.3 154.9 %all-reduce.4.cloned.1.call-start = ((), (), s32[]{:S(2)}) async-start(), calls=%async_computation.2 | async-start | bytes 524288 | tf_op jit(solution)/shard_map/psum | solution.py:28
  7.3 10.4 %copy-start = (f32[16128,128]{1,0:T(8,128)S(1)}, f32[16128,128]{1,0:T(8,128)}, u32[]{:S(2)}) copy-start(f32[16128,128]{1,0:T(8,128)} %param.7) | copy-start | bytes 24772612
  66.1 96.1 %copy-start.3 = (f32[8,64,128]{2,1,0:T(8,128)S(1)}, f32[8,64,128]{2,1,0:T(8,128)}, u32[]{:S(2)}) copy-start(f32[8,64,128]{2,1,0:T(8,128)} %param.5) | copy-start | bytes 786436
  74.2 111.6 %all-gather.5.cloned.1.call-start = ((), (), s32[]{:S(2)}) async-start(), calls=%async_computation.1 | async-start | bytes 2621440 | tf_op jit(solution)/shard_map/all_gather | solution.py:16
  162.1 43.4 %copy-start.8 = (f32[64,128]{1,0:T(8,128)S(1)}, f32[64,128]{1,0:T(8,128)}, u32[]{:S(2)}) copy-start(f32[64,128]{1,0:T(8,128)} %get-tuple-element.8) | copy-start | bytes 98308
  168.4 44.3 %copy-start.7 = (f32[64,128]{1,0:T(8,128)S(1)}, f32[64,128]{1,0:T(8,128)}, u32[]{:S(2)}) copy-start(f32[64,128]{1,0:T(8,128)} %get-tuple-element.9) | copy-start | bytes 98308
  185.8 19.7 %copy-start.1 = (f32[8,64,2048]{2,1,0:T(8,128)S(1)}, f32[8,64,2048]{2,1,0:T(8,128)}, u32[]{:S(2)}) copy-start(f32[8,64,2048]{2,1,0:T(8,128)} %all-gather.3.cloned.1.call-done) | copy-start | bytes 12582916
  185.8 26.5 %copy-start.2 = (f32[8,256,256]{2,1,0:T(8,128)S(1)}, f32[8,256,256]{2,1,0:T(8,128)}, u32[]{:S(2)}) copy-start(f32[8,256,256]{2,1,0:T(8,128)} %all-gather.5.cloned.1.call-done) | copy-start | bytes 6291460
  195.0 24.8 %copy-start.6 = (f32[64,128]{1,0:T(8,128)S(1)}, f32[64,128]{1,0:T(8,128)}, u32[]{:S(2)}) copy-start(f32[64,128]{1,0:T(8,128)} %get-tuple-element.10) | copy-start | bytes 98308
  198.7 28.2 %copy-start.5 = (f32[64,128]{1,0:T(8,128)S(1)}, f32[64,128]{1,0:T(8,128)}, u32[]{:S(2)}) copy-start(f32[64,128]{1,0:T(8,128)} %get-tuple-element.11) | copy-start | bytes 98308
  206.7 27.4 %copy-start.4 = (f32[64,128]{1,0:T(8,128)S(1)}, f32[64,128]{1,0:T(8,128)}, u32[]{:S(2)}) copy-start(f32[64,128]{1,0:T(8,128)} %get-tuple-element.12) | copy-start | bytes 98308
Sparse Core Ops, SparseCore 0:
  9.4 77.7 all-gather.2
  91.4 70.6 all-reduce.3
  163.8 21.9 all-gather.4
where the time goes:
time: 253 us; the launch traced here: 249 us
  waiting for transfers between devices  105 us (42%)
  matrix products  83.6 us (33%)
  blocking collectives  43.7 us (17%)
  between operations  13.6 us (5%)
    psum x1, waiting for transfers between devices, local(): earlier_here = lax.psum(earlier_part, 'pcol')  73.8 us
    dot_general x8, matrix products, local(): jnp.dot(lower_prev[row_block], solved_prev, precision=highest, preferred_...  66.9 us
    all_gather x8, blocking collectives, local(): residual = lax.all_gather(local_residual, 'prow', axis=0, tiled=True)  43.7 us
    all_gather x1, waiting for transfers between devices, local(): full_inverse = lax.all_gather(inverse_diag, 'prow', axis=1, tiled=True)  17.4 us
    all_gather x1, waiting for transfers between devices, local(): full_window = lax.all_gather(lower_window, 'pcol', axis=2, tiled=True)  12.2 us
    dot_general x7, matrix products, local(): jnp.dot(full_window[row_block], solved, precision=highest, preferred_elem...  10.4 us
    dot_general x8, matrix products, local(): jnp.dot(full_inverse[row_block], residual, precision=highest, preferred_e...  6.33 us
  transfers between devices with their start and end apart: 3, of which 3 were waited for; matrix products, arithmetic and copies ran while one was open for 28% of the time, Pallas kernels for 0%

commit v1 on v0

--- a/solution.py
+++ b/solution.py
@@ -13,7 +13,12 @@
     row_start = lax.axis_index("prow") * local_rows
     solved = jnp.zeros((blocks * block_rows, columns), jnp.float32)
     pieces = []
-    full_inverse = lax.all_gather(inverse_diag, "prow", axis=1, tiled=True)
+    ring = [inverse_diag]
+    for hop in range(3):
+        ring.append(lax.ppermute(ring[-1], "prow", [(dev, (dev + 1) % 4) for dev in range(4)]))
+    full_inverse = jnp.roll(
+        jnp.concatenate(ring[::-1], axis=1), (lax.axis_index("prow") + 1) * ring[0].shape[1], axis=1
+    )
     full_window = lax.all_gather(lower_window, "pcol", axis=2, tiled=True)
     for row_block in range(blocks):
         window_term = jnp.dot(

time: 253 us -> 237 us (0.937)
  waiting for transfers between devices: 105 us -> 77.1 us
  local copies, waits for them, and re-layouts: 1.71 us -> 8.32 us
  starting transfers between devices: 0.08 us -> 3.5 us
    all_gather x1 -> x0, waiting for transfers between devices: 17.4 us -> none  [local(): full_inverse = lax.all_gather(inverse_diag, 'prow', axis=1, tiled=True)]
    all_gather x1, waiting for transfers between devices: 12.2 us -> 2.17 us  [local(): full_window = lax.all_gather(lower_window, 'pcol', axis=2, tiled=True)]
    unnamed x25 -> x34, local copies, waits for them, and re-layouts: 0.64 us -> 6.77 us
    dot_general x8, matrix products: 6.33 us -> 10.6 us  [local(): jnp.dot(full_inverse[row_block], residual, precision=highest, preferred_e...]
    ppermute x0 -> x3, starting transfers between devices: none -> 3.46 us  [local(): lax.ppermute(ring[-1], 'prow', [(dev, (dev + 1) % 4) for dev in range(4)])]
    dot_general x7, matrix products: 10.4 us -> 7.35 us  [local(): jnp.dot(full_window[row_block], solved, precision=highest, preferred_elem...]
  transfers between devices with their start and end apart: 3 -> 5, of which waited for: 3 -> 3; matrix products, arithmetic and copies ran while one was open for 28% -> 32% of each run, Pallas kernels for 0% -> 0%
where the time goes in v1:
time: 237 us; the launch traced here: 233 us
  matrix products  84.8 us (36%)
  waiting for transfers between devices  77.1 us (33%)
  blocking collectives  43.7 us (18%)
  between operations  13.9 us (6%)
  local copies, waits for them, and re-layouts  8.32 us (4%)
  starting transfers between devices  3.5 us (1%)
    psum x1, waiting for transfers between devices, local(): earlier_here = lax.psum(earlier_part, 'pcol')  73.8 us
    dot_general x8, matrix products, local(): jnp.dot(lower_prev[row_block], solved_prev, precision=highest, preferred_...  66.8 us
    all_gather x8, blocking collectives, local(): residual = lax.all_gather(local_residual, 'prow', axis=0, tiled=True)  43.7 us
    dot_general x8, matrix products, local(): jnp.dot(full_inverse[row_block], residual, precision=highest, preferred_e...  10.6 us
    dot_general x7, matrix products, local(): jnp.dot(full_window[row_block], solved, precision=highest, preferred_elem...  7.35 us
    unnamed x34, local copies, waits for them, and re-layouts  6.77 us
  transfers between devices with their start and end apart: 5, of which 3 were waited for; matrix products, arithmetic and copies ran while one was open for 32% of the time, Pallas kernels for 0%

profile of v1, /device:TPU:0, one launch (start us, length us, event | category | flops | bytes accessed | tf_op | source)
XLA Modules:
  0.0 233.5 jit_solution(17388461550440783885)
XLA Ops:
  6.5 0.7 all-gather.2.cloned.1.call-update
  7.8 10.7 %fusion = f32[64,128]{1,0:T(8,128)} fusion(f32[16128,128]{1,0:T(8,128)} %param.7, f32[8,64,16128]{2,1,0:T(8,128)} %param.6), kind=kOutput, calls=%fused_computation | convolution fusion | flops 1585446912 | bytes 12419072 | tf_op jit(solution)/shard_map/dot_general | solution.py:27
  18.6 8.2 %fusion.10 = f32[64,128]{1,0:T(8,128)} fusion(f32[16128,128]{1,0:T(8,128)S(1)} %copy-done, f32[8,64,16128]{2,1,0:T(8,128)} %param.6), kind=kOutput, calls=%fused_computation.10 | convolution fusion | flops 1585446912 | bytes 12419072 | tf_op jit(solution)/shard_map/dot_general | solution.py:27
  26.7 7.9 %fusion.12 = f32[64,128]{1,0:T(8,128)} fusion(f32[16128,128]{1,0:T(8,128)S(1)} %copy-done, f32[8,64,16128]{2,1,0:T(8,128)} %param.6), kind=kOutput, calls=%fused_computation.12 | convolution fusion | flops 1585446912 | bytes 12419072 | tf_op jit(solution)/shard_map/dot_general | solution.py:27
  34.6 8.1 %fusion.14 = f32[64,128]{1,0:T(8,128)} fusion(f32[16128,128]{1,0:T(8,128)S(1)} %copy-done, f32[8,64,16128]{2,1,0:T(8,128)} %param.6), kind=kOutput, calls=%fused_computation.14 | convolution fusion | flops 1585446912 | bytes 12419072 | tf_op jit(solution)/shard_map/dot_general | solution.py:27
  42.8 7.9 %fusion.2 = f32[64,128]{1,0:T(8,128)} fusion(f32[16128,128]{1,0:T(8,128)S(1)} %copy-done, f32[8,64,16128]{2,1,0:T(8,128)} %param.6), kind=kOutput, calls=%fused_computation.2 | convolution fusion | flops 1585446912 | bytes 12419072 | tf_op jit(solution)/shard_map/dot_general | solution.py:27
  50.7 8.2 %fusion.4 = f32[64,128]{1,0:T(8,128)} fusion(f32[16128,128]{1,0:T(8,128)S(1)} %copy-done, f32[8,64,16128]{2,1,0:T(8,128)} %param.6), kind=kOutput, calls=%fused_computation.4 | convolution fusion | flops 1585446912 | bytes 12419072 | tf_op jit(solution)/shard_map/dot_general | solution.py:27
  58.9 2.4 %collective-permute-start.1 = (f32[8,64,256]{2,1,0:T(8,128)S(1)}, f32[8,64,256]{2,1,0:T(8,128)S(1)}, u32[]{:S(2)}, u32[]{:S(2)}) collective-permute-start(f32[8,64,256]{2,1,0:T(8,128)S(1)} %collective-permute-done), channel_id=1, source_target_pairs={{0,8},{8,16},{16,24},{24,0},{1,9},{9,17},{17,25},{25,1},{2,10},{10... | collective-permute-start | bytes 1572872 | tf_op jit(solution)/shard_map/ppermute | solution.py:18
  61.2 7.9 %fusion.6 = f32[64,128]{1,0:T(8,128)} fusion(f32[16128,128]{1,0:T(8,128)S(1)} %copy-done, f32[8,64,16128]{2,1,0:T(8,128)} %param.6), kind=kOutput, calls=%fused_computation.6 | convolution fusion | flops 1585446912 | bytes 12419072 | tf_op jit(solution)/shard_map/dot_general | solution.py:27
  69.1 0.6 collective-permute-start.2
  69.7 7.9 %fusion.8 = f32[64,128]{1,0:T(8,128)} fusion(f32[16128,128]{1,0:T(8,128)S(1)} %copy-done, f32[8,64,16128]{2,1,0:T(8,128)} %param.6), kind=kOutput, calls=%fused_computation.8 | convolution fusion | flops 1585446912 | bytes 12419072 | tf_op jit(solution)/shard_map/dot_general | solution.py:27
  78.1 0.9 constant_dynamic-update-slice_fusion.7
  79.0 0.9 constant_dynamic-update-slice_fusion.6
  79.9 0.8 constant_dynamic-update-slice_fusion.5
  80.7 0.9 constant_dynamic-update-slice_fusion.4
  81.6 0.8 constant_dynamic-update-slice_fusion.3
  82.4 0.8 constant_dynamic-update-slice_fusion.2
  83.2 0.9 constant_dynamic-update-slice_fusion.1
  84.1 0.9 constant_dynamic-update-slice_fusion
  85.0 2.2 all-gather.2.cloned.1.call-done
  87.1 1.2 fusion.38
  88.3 73.8 %all-reduce.4.cloned.1.call-done = (f32[64,128]{1,0:T(8,128)}, f32[64,128]{1,0:T(8,128)}, f32[64,128]{1,0:T(8,128)}, f32[64,128]{1,0:T(8,128)}, f32[64,128]{1,0:...) async-done(((f32[64,128]{1,0:T(8,128)}, f32[64,128]{1,0:T(8,128)}, f32[64,128]{1,0:T(8,128)}, f32[64,128]{1,0:T(8,128)}, f32[64,128]{1,0:T(8,128)}, ...) | async-done | bytes 262160 | tf_op jit(solution)/shard_map/psum | solution.py:33
  162.1 1.0 bitcast_subtract_fusion
  163.1 5.6 %all_gather.28 = f32[256,128]{1,0:T(8,128)S(1)} all-gather(f32[64,128]{1,0:T(8,128)S(1)} %bitcast_subtract_fusion), channel_id=1, replica_groups=mesh['prow'=4,'pcol'=8] {'prow'}, dimensions={0}, use_global_device_ids=true | all-gather | bytes 163840 | tf_op jit(solution)/shard_map/all_gather | solution.py:35
  168.7 1.3 fusion.47
  170.1 1.6 fusion.25
  171.7 5.4 %all_gather.29 = f32[256,128]{1,0:T(8,128)S(1)} all-gather(f32[64,128]{1,0:T(8,128)S(1)} %fusion.25), channel_id=1, replica_groups=mesh['prow'=4,'pcol'=8] {'prow'}, dimensions={0}, use_global_device_ids=true | all-gather | bytes 163840 | tf_op jit(solution)/shard_map/all_gather | solution.py:35
  177.1 1.3 constant_dynamic-update-slice_fusion.21
  178.5 1.8 fusion.27
  180.3 5.4 %all_gather.30 = f32[256,128]{1,0:T(8,128)S(1)} all-gather(f32[64,128]{1,0:T(8,128)S(1)} %fusion.27), channel_id=1, replica_groups=mesh['prow'=4,'pcol'=8] {'prow'}, dimensions={0}, use_global_device_ids=true | all-gather | bytes 163840 | tf_op jit(solution)/shard_map/all_gather | solution.py:35
  185.7 1.3 constant_dynamic-update-slice_fusion.20
  187.1 0.8 fusion.29
  187.9 5.4 %all_gather.31 = f32[256,128]{1,0:T(8,128)S(1)} all-gather(f32[64,128]{1,0:T(8,128)S(1)} %fusion.29), channel_id=1, replica_groups=mesh['prow'=4,'pcol'=8] {'prow'}, dimensions={0}, use_global_device_ids=true | all-gather | bytes 163840 | tf_op jit(solution)/shard_map/all_gather | solution.py:35
  193.3 1.3 constant_dynamic-update-slice_fusion.19
  194.6 0.8 fusion.31
  195.4 5.6 %all_gather.32 = f32[256,128]{1,0:T(8,128)S(1)} all-gather(f32[64,128]{1,0:T(8,128)S(1)} %fusion.31), channel_id=1, replica_groups=mesh['prow'=4,'pcol'=8] {'prow'}, dimensions={0}, use_global_device_ids=true | all-gather | bytes 163840 | tf_op jit(solution)/shard_map/all_gather | solution.py:35
  201.0 1.3 constant_dynamic-update-slice_fusion.18
  202.3 0.8 fusion.33
  203.1 5.4 %all_gather.33 = f32[256,128]{1,0:T(8,128)S(1)} all-gather(f32[64,128]{1,0:T(8,128)S(1)} %fusion.33), channel_id=1, replica_groups=mesh['prow'=4,'pcol'=8] {'prow'}, dimensions={0}, use_global_device_ids=true | all-gather | bytes 163840 | tf_op jit(solution)/shard_map/all_gather | solution.py:35
  208.6 1.3 constant_dynamic-update-slice_fusion.17
  209.9 0.8 fusion.35
  210.7 5.4 %all_gather.34 = f32[256,128]{1,0:T(8,128)S(1)} all-gather(f32[64,128]{1,0:T(8,128)S(1)} %fusion.35), channel_id=1, replica_groups=mesh['prow'=4,'pcol'=8] {'prow'}, dimensions={0}, use_global_device_ids=true | all-gather | bytes 163840 | tf_op jit(solution)/shard_map/all_gather | solution.py:35
  216.1 1.3 constant_dynamic-update-slice_fusion.16
  217.5 0.8 fusion.37
  218.2 5.4 %all_gather.35 = f32[256,128]{1,0:T(8,128)S(1)} all-gather(f32[64,128]{1,0:T(8,128)S(1)} %fusion.37), channel_id=1, replica_groups=mesh['prow'=4,'pcol'=8] {'prow'}, dimensions={0}, use_global_device_ids=true | all-gather | bytes 163840 | tf_op jit(solution)/shard_map/all_gather | solution.py:35
  223.7 1.3 fusion.40
  225.1 0.7 copy-done.9
  225.8 0.6 constant_dynamic-update-slice_fusion.8
  (34 shorter events, 1.2 us)
Async XLA Ops:
  6.5 80.6 %all-gather.2.cloned.1.call-start = ((), (), s32[]{:S(2)}) async-start(), calls=%async_computation | async-start | bytes 4718592 | tf_op jit(solution)/shard_map/all_gather | solution.py:22
  7.3 154.9 %all-reduce.4.cloned.1.call-start = ((), (), s32[]{:S(2)}) async-start(), calls=%async_computation.1 | async-start | bytes 524288 | tf_op jit(solution)/shard_map/psum | solution.py:33
  7.3 11.2 %copy-start = (f32[16128,128]{1,0:T(8,128)S(1)}, f32[16128,128]{1,0:T(8,128)}, u32[]{:S(2)}) copy-start(f32[16128,128]{1,0:T(8,128)} %param.7) | copy-start | bytes 24772612
  7.3 51.6 %collective-permute-start = (f32[8,64,256]{2,1,0:T(8,128)}, f32[8,64,256]{2,1,0:T(8,128)S(1)}, u32[]{:S(2)}, u32[]{:S(2)}) collective-permute-start(f32[8,64,256]{2,1,0:T(8,128)} %param.9), channel_id=1, source_target_pairs={{0,8},{8,16},{16,24},{24,0},{1,9},{9,17},{17,25},{25,1},{2,10},{10... | collective-permute-start | bytes 1572872 | tf_op jit(solution)/shard_map/ppermute | solution.py:18
  58.9 10.3 %collective-permute-start.1 = (f32[8,64,256]{2,1,0:T(8,128)S(1)}, f32[8,64,256]{2,1,0:T(8,128)S(1)}, u32[]{:S(2)}, u32[]{:S(2)}) collective-permute-start(f32[8,64,256]{2,1,0:T(8,128)S(1)} %collective-permute-done), channel_id=1, source_target_pairs={{0,8},{8,16},{16,24},{24,0},{1,9},{9,17},{17,25},{25,1},{2,10},{10... | collective-permute-start | bytes 1572872 | tf_op jit(solution)/shard_map/ppermute | solution.py:18
  69.1 11.6 %copy-start.2 = (f32[8,64,256]{2,1,0:T(8,128)S(1)}, f32[8,64,256]{2,1,0:T(8,128)}, u32[]{:S(2)}) copy-start(f32[8,64,256]{2,1,0:T(8,128)} %param.9) | copy-start | bytes 1572868
  69.1 9.0 %collective-permute-start.2 = (f32[8,64,256]{2,1,0:T(8,128)S(1)}, f32[8,64,256]{2,1,0:T(8,128)S(1)}, u32[]{:S(2)}, u32[]{:S(2)}) collective-permute-start(f32[8,64,256]{2,1,0:T(8,128)S(1)} %collective-permute-done.1), channel_id=1, source_target_pairs={{0,8},{8,16},{16,24},{24,0},{1,9},{9,17},{17,25},{25,1},{2,10},{10... | collective-permute-start | bytes 1572872 | tf_op jit(solution)/shard_map/ppermute | solution.py:18
  79.0 83.1 %copy-start.3 = (f32[8,64,128]{2,1,0:T(8,128)S(1)}, f32[8,64,128]{2,1,0:T(8,128)}, u32[]{:S(2)}) copy-start(f32[8,64,128]{2,1,0:T(8,128)} %param.5) | copy-start | bytes 786436
  162.1 24.9 %copy-start.1 = (f32[8,64,2048]{2,1,0:T(8,128)S(1)}, f32[8,64,2048]{2,1,0:T(8,128)}, u32[]{:S(2)}) copy-start(f32[8,64,2048]{2,1,0:T(8,128)} %all-gather.2.cloned.1.call-done) | copy-start | bytes 12582916
  162.1 24.9 %copy-start.8 = (f32[64,128]{1,0:T(8,128)S(1)}, f32[64,128]{1,0:T(8,128)}, u32[]{:S(2)}) copy-start(f32[64,128]{1,0:T(8,128)} %get-tuple-element.8) | copy-start | bytes 98308
  163.1 31.5 %copy-start.7 = (f32[64,128]{1,0:T(8,128)S(1)}, f32[64,128]{1,0:T(8,128)}, u32[]{:S(2)}) copy-start(f32[64,128]{1,0:T(8,128)} %get-tuple-element.9) | copy-start | bytes 98308
  171.7 30.6 %copy-start.6 = (f32[64,128]{1,0:T(8,128)S(1)}, f32[64,128]{1,0:T(8,128)}, u32[]{:S(2)}) copy-start(f32[64,128]{1,0:T(8,128)} %get-tuple-element.10) | copy-start | bytes 98308
  180.3 29.6 %copy-start.5 = (f32[64,128]{1,0:T(8,128)S(1)}, f32[64,128]{1,0:T(8,128)}, u32[]{:S(2)}) copy-start(f32[64,128]{1,0:T(8,128)} %get-tuple-element.11) | copy-start | bytes 98308
  187.8 29.6 %copy-start.4 = (f32[64,128]{1,0:T(8,128)S(1)}, f32[64,128]{1,0:T(8,128)}, u32[]{:S(2)}) copy-start(f32[64,128]{1,0:T(8,128)} %get-tuple-element.12) | copy-start | bytes 98308
  225.1 0.7 copy-start.9
Sparse Core Ops, SparseCore 0:
  9.4 77.7 all-gather.1
  91.4 70.6 all-reduce.3
